TPU v7x, 32 devices: a whole 2x2x4 slice. The times are simulated.
32 devices in a mesh: tm: 4 (over x, core), cell: 8 (over z, y).
Axes of the slice: x: 2, y: 2, z: 4, core: 2. Of those that a mesh axis runs over, the one named last changes fastest.
Arguments:
- sensitivity: bfloat16 [2048, 4, 4096], P(None, 'tm', 'cell'), may hold values from -0.1875 to 0.1875
- duals: bfloat16 [2048, 128], P(('tm', 'cell')), may hold values from -6 to 6
- time_cov: float32 [4, 4], replicated, may hold values from 0.05 to 0.5
- cell_coords: int32 [2, 4096], P(None, 'cell'), may hold values from 0 to 127, as said below
- obs_time: int32 [2048], replicated, may hold values from 0 to 3
- obs_owner: int32 [2048], replicated, may hold values from 0 to 2047, each once
Outputs:
- product: float32 [2048, 128], P(('tm', 'cell'))
Inputs may be any that keep to these rules, and one draw needn't show every extreme that they name: `cell_coords`: every cell has its own grid position; rows lie below 32 and columns below 128. `obs_owner`: every observation stands in exactly one slot.
All inputs are finite; a program needn't handle non-finite values.
Results may differ from a plain program's by a relative error of at most 0.0049.
Values may be sent and summed in bfloat16 or wider, within the bound.
A program may use at most 64 MiB of HBM per device.

v0:
```python
import functools

import jax
import jax.numpy as jnp
from jax import lax
from jax.experimental import pallas as pl
from jax.experimental.pallas import tpu as pltpu
from jax.sharding import PartitionSpec as P

LSCALE = 4
LANES = 128
HALVES = 2
PICK_ROWS = 256
QUARTERS = 4
FILL = (0, 3, 3, 1, 1)
MESH = pl.DeviceIdType.MESH
BF16 = jnp.bfloat16
F32 = jnp.float32


def remote(src, dst, sems, index, device):
    send, recv = sems
    return pltpu.make_async_remote_copy(
        src_ref=src, dst_ref=dst, send_sem=send.at[index], recv_sem=recv.at[index],
        device_id=device, device_id_type=MESH,
    )


def column_of(row):
    return jnp.broadcast_to(row, (LANES, row.shape[1])).T


def kernel(cfg, sens_hbm, duals_ref, cov_ref, coords_ref, time_ref, owner_ref, out_ref, *s):
    n_hi, n_cell, gather, scatter = cfg
    n_tm = 2 * n_hi
    (sens, full, coords_all, mask_t, picked, row_b, col_b, own_b, ids, cov_k, adj, held, acc,
     core_out, core_in, x_out, x_in, total, cell_out, cell_in, local_sem, *pairs) = s
    co, ac, ax, ap, bx, bp, ring_r, ring_l, dp, dx, dc = zip(pairs[0::2], pairs[1::2])
    obs, cells = sens.shape
    rows = duals_ref.shape[0]
    half = cells // HALVES
    quarter = cells // QUARTERS

    tm = lax.axis_index("tm")
    cell = lax.axis_index("cell")
    hi, core = tm // 2, tm % 2
    partner = (hi * 2 + (1 - core), cell)

    def hi_at(q):
        return lax.rem(hi + q + n_hi, n_hi)

    def x_peer(q):
        return (hi_at(q) * 2 + core, cell)

    def cell_at(k):
        return lax.rem(cell + k + n_cell, n_cell)

    load = pltpu.make_async_copy(sens_hbm, sens, local_sem)
    load.start()

    barrier = pltpu.get_barrier_semaphore()
    peers = [(tm, cell_at(k)) for k in range(1, n_cell)] + [x_peer(q) for q in range(1, n_hi)] + [partner]
    for peer in peers:
        pl.semaphore_signal(barrier, inc=1, device_id=peer, device_id_type=MESH)
    coords_all[cell] = coords_ref[...]
    row_b[...] = column_of(coords_ref[0:1, :].astype(F32))
    col_b[...] = column_of(coords_ref[1:2, :].astype(F32))
    own_b[...] = column_of(owner_ref[...].astype(F32))
    live = tm <= time_ref[...]
    ids[...] = jnp.where(live, lax.broadcasted_iota(jnp.int32, (1, obs), 1), -1).astype(F32)

    def covariance_block(c):
        @pl.loop(0, cells // LANES)
        def _(j):
            lanes = pl.ds(pl.multiple_of(j * LANES, LANES), LANES)
            row_gap = row_b[...] - coords_all[c, 0:1, lanes].astype(F32)
            col_gap = col_b[...] - coords_all[c, 1:2, lanes].astype(F32)
            distance = jnp.sqrt(row_gap * row_gap + col_gap * col_gap)
            cov_k[c, :, lanes] = (jnp.exp(-distance / LSCALE) / (8.0 * LSCALE)).astype(BF16)

    def pick(i):
        at = slice(i * PICK_ROWS, (i + 1) * PICK_ROWS)
        owned = own_b[at, :]
        hot = [
            jnp.where(owned == ids[:, j * LANES:(j + 1) * LANES], 1.0, 0.0).astype(BF16)
            for j in range(obs // LANES)
        ]
        picked[at, :] = jnp.dot(
            jnp.concatenate(hot, axis=1), sens[...], preferred_element_type=F32
        ).astype(BF16)

    fillers = [functools.partial(pick, i) for i in range(obs // PICK_ROWS)]

    def fill(count):
        for _ in range(count):
            if fillers:
                fillers.pop(0)()

    covariance_block(cell)
    load.wait()

    @pl.loop(0, obs // PICK_ROWS)
    def _(i):
        at = pl.ds(pl.multiple_of(i * PICK_ROWS, PICK_ROWS), PICK_ROWS)
        alive = jnp.where(ids[:, at] >= 0.0, 1.0, 0.0).astype(BF16)
        mask_t[:, at] = sens[at, :].T * alive

    fill(FILL[0])
    pl.semaphore_wait(barrier, len(peers))

    sent = []

    def go(copy):
        copy.start()
        sent.append(copy)
        return copy

    co_copies = {}
    for k in range(1, n_cell):
        co_copies[k] = go(remote(coords_ref, coords_all.at[cell], co, k, (tm, cell_at(k))))

    def block(t, c):
        return full.at[t * n_cell + c]

    cell_copies, x_copies, core_copies = {}, {}, {}

    def forward_x(src, k):
        for q in range(1, n_hi):
            x_copies[q, k] = go(remote(src, block(tm, cell_at(-k)), ax, q * n_cell + k, x_peer(q)))

    def forward_core(src, q, k):
        dst = block(hi_at(-q) * 2 + core, cell_at(-k))
        core_copies[q, k] = go(remote(src, dst, ap, q * n_cell + k, partner))

    if gather:
        for k in range(1, n_cell):
            cell_copies[k] = go(remote(duals_ref, block(tm, cell), ac, k, (tm, cell_at(k))))
        forward_x(duals_ref, 0)
        forward_core(duals_ref, 0, 0)
        full[tm * n_cell + cell] = duals_ref[...]

    fill(FILL[1])
    for k in range(1, n_cell):
        if gather:
            cell_copies[k].wait_recv()
            src = block(tm, cell_at(-k))
            forward_x(src, k)
            forward_core(src, 0, k)
    fill(FILL[2])
    if gather:
        for k in range(n_cell):
            for q in range(1, n_hi):
                x_copies[q, k].wait_recv()
                forward_core(block(hi_at(-q) * 2 + core, cell_at(-k)), q, k)
    for k in range(1, n_cell):
        co_copies[k].wait_recv()
    if gather:
        for k in range(n_cell):
            for q in range(n_hi):
                core_copies[q, k].wait_recv()

    bx_copies, bp_copies = {}, {}
    for h in range(HALVES):
        at = slice(h * half, (h + 1) * half)
        everything = full[...].reshape(obs, LANES) if gather else duals_ref[...]
        adj[tm, at, :] = jnp.dot(mask_t[at, :], everything, preferred_element_type=F32).astype(BF16)
        here = adj.at[tm, at]
        for q in range(1, n_hi):
            bx_copies[q, h] = go(remote(here, here, bx, q * HALVES + h, x_peer(q)))
        bp_copies[0, h] = go(remote(here, here, bp, h, partner))

    fill(FILL[3])
    for h in range(HALVES):
        for q in range(1, n_hi):
            bx_copies[q, h].wait_recv()
            got = adj.at[hi_at(-q) * 2 + core, h * half:(h + 1) * half]
            bp_copies[q, h] = go(remote(got, got, bp, q * HALVES + h, partner))
    fill(FILL[4])

    major = cell // 2
    place = jnp.where(cell % 2 == 0, major, n_cell - 1 - major)

    def cell_on(k):
        p = lax.rem(place + k + n_cell, n_cell)
        return jnp.where(p < n_cell // 2, p * 2, (n_cell - 1 - p) * 2 + 1)

    steps = n_cell // 2
    ring = {}

    def carries(way, step, h):
        return step < steps or (step == steps and (h < QUARTERS // 2) == (way > 0))

    def ring_send(way, step, h):
        if carries(way, step, h):
            part = held.at[cell_on(-way * (step - 1)), h * quarter:(h + 1) * quarter]
            sems = ring_r if way > 0 else ring_l
            ring[way, step, h] = go(remote(part, part, sems, step * QUARTERS + h, (tm, cell_on(way))))

    per_half = QUARTERS // HALVES
    for h in range(HALVES):
        at = slice(h * half, (h + 1) * half)
        for q in range(n_hi):
            bp_copies[q, h].wait_recv()
        mixed = cov_ref[tm, 0] * adj[0, at, :].astype(F32)
        for t in range(1, n_tm):
            mixed += cov_ref[tm, t] * adj[t, at, :].astype(F32)
        held[cell, at, :] = mixed.astype(BF16)
        for piece in range(h * per_half, (h + 1) * per_half):
            ring_send(1, 1, piece)
            ring_send(-1, 1, piece)

    def spread(c):
        return jnp.dot(cov_k[c], held[c], preferred_element_type=F32)

    def blocks(step):
        return [cell_on(-step), cell_on(step)] if step < steps else [cell_on(step)]

    acc[...] = spread(cell)
    for c in blocks(1):
        covariance_block(c)
    for step in range(1, steps + 1):
        for h in range(QUARTERS):
            for way in (1, -1):
                if carries(way, step, h):
                    ring[way, step, h].wait_recv()
                    ring_send(way, step + 1, h)
            if step < steps and h < len(blocks(step + 1)):
                covariance_block(blocks(step + 1)[h])
        for c in blocks(step):
            acc[...] += spread(c)
    fill(len(fillers))

    weighted = acc[...].astype(BF16)
    if scatter:
        span = rows * n_cell

        def product(t):
            at = pl.ds(pl.multiple_of(t * span, span), span)
            return jnp.dot(picked[at, :], weighted, preferred_element_type=F32)

        dp_copies, dx_copies, dc_copies = {}, {}, {}
        order = [*range(1, n_hi), 0]
        for q in order:
            core_out[q] = product(hi_at(q) * 2 + (1 - core)).astype(BF16)
            dp_copies[q] = go(remote(core_out.at[q], core_in.at[q], dp, q, partner))
        far = sorted(range(n_cell), key=lambda k: -min(k, n_cell - k))
        for q in order:
            summed = product(hi_at(q) * 2 + core)
            dp_copies[q].wait_recv()
            total[...] = (summed + core_in[q].astype(F32)).reshape(n_cell, rows, LANES)
            if q:
                for k in far:
                    c = cell_at(k)
                    x_out[q, c] = total[c].astype(BF16)
                    dx_copies[q, k] = go(remote(x_out.at[q, c], x_in.at[q, c], dx, q * n_cell + k, x_peer(q)))
        for k in far:
            c = cell_at(k)
            block_sum = total[c]
            for q in range(1, n_hi):
                dx_copies[q, k].wait_recv()
                block_sum += x_in[q, c].astype(F32)
            if k:
                cell_out[c] = block_sum.astype(BF16)
                dc_copies[k] = go(remote(cell_out.at[c], cell_in.at[k], dc, k, (tm, c)))
        result = block_sum
        for k in range(1, n_cell):
            dc_copies[k].wait_recv()
            result += cell_in[k].astype(F32)
        out_ref[...] = result
    else:
        for i in range(obs // PICK_ROWS):
            at = slice(i * PICK_ROWS, (i + 1) * PICK_ROWS)
            out_ref[at, :] = jnp.dot(picked[at, :], weighted, preferred_element_type=F32)

    for copy in sent:
        copy.wait_send()


def per_device(n_tm, n_cell, sensitivity, duals, time_cov, cell_coords, obs_time, obs_owner):
    obs, _, cells = sensitivity.shape
    rows, reals = duals.shape
    n_hi = n_tm // 2
    inside = rows % 16 == 0
    if not inside:
        duals = lax.all_gather(duals, ("tm", "cell"), axis=0, tiled=True)
    span = rows * n_cell if inside else 16
    part = rows if inside else 16
    vmem = pl.BlockSpec(memory_space=pltpu.VMEM)

    def pair(count):
        return [pltpu.SemaphoreType.DMA((count,)), pltpu.SemaphoreType.DMA((count,))]

    steps = n_cell // 2 + 1
    out_rows = rows if inside else obs
    out = pl.pallas_call(
        functools.partial(kernel, (n_hi, n_cell, inside, inside)),
        out_shape=jax.ShapeDtypeStruct((out_rows, reals), F32),
        in_specs=[
            pl.BlockSpec(memory_space=pl.ANY), vmem, pl.BlockSpec(memory_space=pltpu.SMEM), vmem, vmem, vmem,
        ],
        out_specs=vmem,
        scratch_shapes=[
            pltpu.VMEM((obs, cells), BF16),
            pltpu.VMEM((n_tm * n_cell if inside else 1, part, reals), BF16),
            pltpu.VMEM((n_cell, 2, cells), jnp.int32),
            pltpu.VMEM((cells, obs), BF16),
            pltpu.VMEM((obs, cells), BF16),
            pltpu.VMEM((cells, LANES), F32),
            pltpu.VMEM((cells, LANES), F32),
            pltpu.VMEM((obs, LANES), F32),
            pltpu.VMEM((1, obs), F32),
            pltpu.VMEM((n_cell, cells, cells), BF16),
            pltpu.VMEM((n_tm, cells, reals), BF16),
            pltpu.VMEM((n_cell, cells, reals), BF16),
            pltpu.VMEM((cells, reals), F32),
            pltpu.VMEM((n_hi, span, reals), BF16),
            pltpu.VMEM((n_hi, span, reals), BF16),
            pltpu.VMEM((n_hi, n_cell, part, reals), BF16),
            pltpu.VMEM((n_hi, n_cell, part, reals), BF16),
            pltpu.VMEM((n_cell, part, reals), F32),
            pltpu.VMEM((n_cell, part, reals), BF16),
            pltpu.VMEM((n_cell, part, reals), BF16),
            pltpu.SemaphoreType.DMA,
            *pair(n_cell), *pair(n_cell), *pair(n_hi * n_cell), *pair(n_hi * n_cell),
            *pair(n_hi * HALVES), *pair(n_hi * HALVES),
            *pair(steps * QUARTERS), *pair(steps * QUARTERS),
            *pair(n_hi), *pair(n_hi * n_cell), *pair(n_cell),
        ],
        compiler_params=pltpu.CompilerParams(
            collective_id=0, has_side_effects=True, vmem_limit_bytes=62 * 1024 * 1024
        ),
    )(
        sensitivity.reshape(obs, cells), duals, time_cov, cell_coords,
        obs_time.reshape(1, obs), obs_owner.reshape(1, obs),
    )
    if inside:
        return out
    return lax.psum_scatter(out, ("tm", "cell"), scatter_dimension=0, tiled=True)


def solution(mesh):
    in_specs = (P(None, "tm", "cell"), P(("tm", "cell"), None), P(), P(None, "cell"), P(), P())
    out_specs = P(("tm", "cell"), None)
    return jax.shard_map(
        functools.partial(per_device, mesh.shape["tm"], mesh.shape["cell"]),
        mesh=mesh, in_specs=in_specs, out_specs=out_specs, check_vma=False,
    )
```

profile of v0, /device:TPU:0, one launch (start us, length us, event | category | flops | bytes accessed | tf_op | source)
XLA Modules:
  0.0 51.4 jit_solution(17254248384924954672)
XLA Ops:
  0.0 50.0 %shard_map.64 = f32[64,128]{1,0:T(8,128)} custom-call(bf16[2048,512]{1,0:T(8,128)(2,1)} %bitcast.3, bf16[64,128]{1,0:T(8,128)(2,1)} %duals_ref.1, f32[4,4]{1,0:T(4,128)} %cov_ref.1, s32[2,512]{1,0:T(2,128)} %coords_ref.1, s32[1,2048]{1,0:T(1,128)} %bitcast.4, s32[1,2048]{1,0:T(1,128)} %bitcast.5), custom_call_target="tpu_custom_call" | custom-call | tf_op jit(solution)/shard_map/pallas_call | solution.py:295
  50.1 1.4 %copy.8 = f32[64,128]{1,0:T(8,128)} copy(f32[64,128]{1,0:T(8,128)} %shard_map.64) | data formatting | bytes 65536
where the time goes:
time: 51.7 us; the launch traced here: 51.4 us
  Pallas kernels  50 us (97%)
  local copies, waits for them, and re-layouts  1.38 us (3%)
    pallas_call x1, Pallas kernels, per_device(): pl.pallas_call(functools.partial(kernel, (n_hi, n_cell, inside, inside)),...  50 us
    unnamed x1, local copies, waits for them, and re-layouts  1.38 us

commit v1 on v0

--- a/solution.py
+++ b/solution.py
@@ -30,7 +30,7 @@
     return jnp.broadcast_to(row, (LANES, row.shape[1])).T
 
 
-def kernel(cfg, sens_hbm, duals_ref, cov_ref, coords_ref, time_ref, owner_ref, out_ref, *s):
+def ring_kernel(cfg, sens_hbm, duals_ref, cov_ref, coords_ref, time_ref, owner_ref, out_ref, *s):
     n_hi, n_cell, gather, scatter = cfg
     n_tm = 2 * n_hi
     (sens, full, coords_all, mask_t, picked, row_b, col_b, own_b, ids, cov_k, adj, held, acc,
@@ -276,7 +276,7 @@
         copy.wait_send()
 
 
-def per_device(n_tm, n_cell, sensitivity, duals, time_cov, cell_coords, obs_time, obs_owner):
+def ring_program(n_tm, n_cell, sensitivity, duals, time_cov, cell_coords, obs_time, obs_owner):
     obs, _, cells = sensitivity.shape
     rows, reals = duals.shape
     n_hi = n_tm // 2
@@ -293,7 +293,7 @@
     steps = n_cell // 2 + 1
     out_rows = rows if inside else obs
     out = pl.pallas_call(
-        functools.partial(kernel, (n_hi, n_cell, inside, inside)),
+        functools.partial(ring_kernel, (n_hi, n_cell, inside, inside)),
         out_shape=jax.ShapeDtypeStruct((out_rows, reals), F32),
         in_specs=[
             pl.BlockSpec(memory_space=pl.ANY), vmem, pl.BlockSpec(memory_space=pltpu.SMEM), vmem, vmem, vmem,
@@ -338,6 +338,358 @@
     return lax.psum_scatter(out, ("tm", "cell"), scatter_dimension=0, tiled=True)
 
 
+GROUP = 4
+PAD = GROUP - 1
+TILE = 16
+
+
+def field_kernel(cfg, sens_hbm, duals_ref, cov_ref, coords_ref, time_ref, owner_ref, out_ref, *s):
+    n_hi, n_cell = cfg
+    n_tm = 2 * n_hi
+    (sens, full, coords_all, mask_t, picked, own_b, ids, toeplitz, hot_t, hot, halves, stage, tiles, fields, mixed,
+     placed, grid, acc, back, outs, returned, weighted, core_out, core_in, x_out, x_in, total, cell_out, cell_in,
+     local_sem, *pairs) = s
+    co, ac, ax, ap, ea, eb, dp, dx, dc = zip(pairs[0::2], pairs[1::2])
+    obs, cells = sens.shape
+    rows = duals_ref.shape[0]
+    blocks = cells // LANES
+    grid_rows = n_cell * cells // LANES
+    duos = grid_rows // 2
+    wide = 2 * LANES
+
+    tm = lax.axis_index("tm")
+    cell = lax.axis_index("cell")
+    hi, core = tm // 2, tm % 2
+    partner = (hi * 2 + (1 - core), cell)
+    me = tm * n_cell + cell
+
+    def hi_at(q):
+        return lax.rem(hi + q + n_hi, n_hi)
+
+    def x_peer(q):
+        return (hi_at(q) * 2 + core, cell)
+
+    def cell_at(k):
+        return lax.rem(cell + k + n_cell, n_cell)
+
+    def tm_at(a):
+        return lax.rem(tm + a + n_tm, n_tm)
+
+    load = pltpu.make_async_copy(sens_hbm, sens, local_sem)
+    load.start()
+
+    barrier = pltpu.get_barrier_semaphore()
+    peers = [(tm, cell_at(k)) for k in range(1, n_cell)] + [x_peer(q) for q in range(1, n_hi)] + [partner]
+    for peer in peers:
+        pl.semaphore_signal(barrier, inc=1, device_id=peer, device_id_type=MESH)
+    coords_all[cell] = coords_ref[...]
+    own_b[...] = column_of(owner_ref[...].astype(F32))
+    live = tm <= time_ref[...]
+    ids[...] = jnp.where(live, lax.broadcasted_iota(jnp.int32, (1, obs), 1), -1).astype(F32)
+
+    col_gap = (
+        lax.broadcasted_iota(jnp.int32, (LANES, LANES), 0) - lax.broadcasted_iota(jnp.int32, (LANES, LANES), 1)
+    ).astype(F32)
+    col_gap = col_gap * col_gap
+    grid[...] = jnp.zeros_like(grid)
+
+    @pl.loop(0, grid_rows)
+    def _(gap):
+        row_gap = gap.astype(F32)
+        distance = jnp.sqrt(row_gap * row_gap + col_gap)
+        block = (jnp.exp(-distance / LSCALE) / (8.0 * LSCALE)).astype(BF16)
+        toeplitz[grid_rows - 1 - gap] = block
+        toeplitz[grid_rows - 1 + gap] = block
+
+    load.wait()
+
+    @pl.loop(0, obs // PICK_ROWS)
+    def _(i):
+        at = pl.ds(pl.multiple_of(i * PICK_ROWS, PICK_ROWS), PICK_ROWS)
+        alive = jnp.where(ids[:, at] >= 0.0, 1.0, 0.0).astype(BF16)
+        mask_t[:, at] = sens[at, :].T * alive
+
+    def pick(i):
+        at = slice(i * PICK_ROWS, (i + 1) * PICK_ROWS)
+        owned = own_b[at, :]
+        hits = [
+            jnp.where(owned == ids[:, j * LANES:(j + 1) * LANES], 1.0, 0.0).astype(BF16)
+            for j in range(obs // LANES)
+        ]
+        picked[at, :] = jnp.dot(
+            jnp.concatenate(hits, axis=1), sens[...], preferred_element_type=F32
+        ).astype(BF16)
+
+    fillers = [functools.partial(pick, i) for i in range(obs // PICK_ROWS)]
+
+    def fill(count):
+        for _ in range(count):
+            if fillers:
+                fillers.pop(0)()
+
+    fill(PLAN[0])
+    pl.semaphore_wait(barrier, len(peers))
+
+    sent = []
+
+    def go(copy):
+        copy.start()
+        sent.append(copy)
+        return copy
+
+    def block_of(t, c):
+        return full.at[t * n_cell + c]
+
+    co_copies, cell_copies, x_copies, core_copies = {}, {}, {}, {}
+
+    def forward_x(src, k):
+        for q in range(1, n_hi):
+            x_copies[q, k] = go(remote(src, block_of(tm, cell_at(-k)), ax, q * n_cell + k, x_peer(q)))
+
+    def forward_core(src, q, k):
+        dst = block_of(hi_at(-q) * 2 + core, cell_at(-k))
+        core_copies[q, k] = go(remote(src, dst, ap, q * n_cell + k, partner))
+
+    for k in range(1, n_cell):
+        cell_copies[k] = go(remote(duals_ref, block_of(tm, cell), ac, k, (tm, cell_at(k))))
+    forward_x(duals_ref, 0)
+    forward_core(duals_ref, 0, 0)
+    for k in range(1, n_cell):
+        co_copies[k] = go(remote(coords_ref, coords_all.at[cell], co, k, (tm, cell_at(k))))
+    full[me] = duals_ref[...]
+
+    fill(PLAN[1])
+    for k in range(1, n_cell):
+        cell_copies[k].wait_recv()
+        src = block_of(tm, cell_at(-k))
+        forward_x(src, k)
+        forward_core(src, 0, k)
+    fill(PLAN[2])
+    for k in range(n_cell):
+        for q in range(1, n_hi):
+            x_copies[q, k].wait_recv()
+            forward_core(block_of(hi_at(-q) * 2 + core, cell_at(-k)), q, k)
+    for k in range(n_cell):
+        for q in range(n_hi):
+            core_copies[q, k].wait_recv()
+
+    reals = duals_ref.shape[1]
+    adjoint = jnp.dot(mask_t[...], full[...].reshape(obs, reals), preferred_element_type=F32)
+    for b in range(blocks):
+        stage[pl.ds(b, reals, stride=blocks), :] = adjoint[b * LANES:(b + 1) * LANES, :].T
+    tiles[...] = stage[...].astype(BF16).reshape(tiles.shape)
+
+    shifts = [(a, k) for k in sorted(range(n_cell), key=lambda k: -min(k, n_cell - k)) for a in range(n_tm)]
+    ea_copies = {}
+    for a, k in shifts:
+        if (a, k) != (0, 0):
+            peer = (tm_at(a), cell_at(k))
+            ea_copies[a, k] = go(
+                remote(tiles.at[peer[0] * n_cell + peer[1]], fields.at[me], ea, a * n_cell + k, peer)
+            )
+    fields[me] = tiles[me]
+
+    for k in range(1, n_cell):
+        co_copies[k].wait_recv()
+    for k in range(n_cell):
+        code = (coords_all[k, 0:1, :] & 1) * LANES + coords_all[k, 1:2, :]
+        spots = lax.broadcasted_iota(jnp.int32, (wide, cells), 0)
+        ones = jnp.where(spots == code, 1.0, 0.0).astype(BF16)
+        hot_t[k] = ones
+        hot[k] = ones.T
+        halves[k] = coords_all[k, 0:1, :] >> 1
+    fill(PLAN[3])
+
+    for copy in ea_copies.values():
+        copy.wait_recv()
+    for k in range(n_cell):
+        got = [fields[t * n_cell + k].astype(F32) for t in range(n_tm)]
+        for t in range(n_tm):
+            blend = cov_ref[t, 0] * got[0]
+            for u in range(1, n_tm):
+                blend += cov_ref[t, u] * got[u]
+            mixed[k, t * TILE:(t + 1) * TILE, :] = blend
+        for b in range(blocks):
+            lanes = slice(b * LANES, (b + 1) * LANES)
+            x = mixed[k, pl.ds(b, TILE, stride=blocks), :]
+            for d in range(duos):
+                placed[k, d * TILE:(d + 1) * TILE, lanes] = jnp.where(halves[k, 0:1, lanes] == d, x, 0.0).astype(BF16)
+    on_grid = jnp.dot(placed[0], hot[0], preferred_element_type=F32)
+    for k in range(1, n_cell):
+        on_grid += jnp.dot(placed[k], hot[k], preferred_element_type=F32)
+    grid[PAD * TILE:(PAD + duos) * TILE, :] = on_grid.astype(BF16)
+
+    def covariance(m):
+        at = grid_rows - 1 - 2 * m
+        left = toeplitz[at:at + 2].reshape(wide, LANES)
+        right = toeplitz[at - 1:at + 1].reshape(wide, LANES)
+        return jnp.concatenate([left, right], axis=1)
+
+    spans = [list(range(m, min(m + GROUP, duos))) for m in range(1 - duos, duos, GROUP)]
+    spans.sort(key=lambda span: 0 not in span)
+    for span in spans:
+        low, high = max(0, span[0]), min(duos, duos + span[-1])
+        count = (high - low) * TILE
+        lhs = jnp.concatenate(
+            [grid[(PAD + low - m) * TILE:(PAD + low - m) * TILE + count, :] for m in span], axis=1
+        )
+        rhs = jnp.concatenate([covariance(m) for m in span], axis=0)
+        term = jnp.dot(lhs, rhs, preferred_element_type=F32)
+        at = slice(low * TILE, high * TILE)
+        if 0 in span:
+            acc[at, :] = term
+        else:
+            acc[at, :] += term
+
+    smooth = acc[...].astype(BF16)
+    eb_copies = {}
+    for k in sorted(range(n_cell), key=lambda k: -min(k, n_cell - k)):
+        c = cell_at(k)
+        spread = jnp.dot(smooth, hot_t[c], preferred_element_type=F32)
+        for b in range(blocks):
+            lanes = slice(b * LANES, (b + 1) * LANES)
+            half = halves[c, 0:1, lanes]
+            found = spread[0:TILE, lanes]
+            for d in range(1, duos):
+                found = jnp.where(half == d, spread[d * TILE:(d + 1) * TILE, lanes], found)
+            back[k, pl.ds(b, TILE, stride=blocks), :] = found
+        for t in range(n_tm):
+            outs[t * n_cell + c] = back[k, t * TILE:(t + 1) * TILE, :].astype(BF16)
+        for a in range(n_tm):
+            if (a, k) != (0, 0):
+                peer = (tm_at(a), c)
+                eb_copies[a, k] = go(
+                    remote(outs.at[peer[0] * n_cell + c], returned.at[me], eb, a * n_cell + k, peer)
+                )
+    returned[me] = outs[me]
+    fill(len(fillers))
+    for copy in eb_copies.values():
+        copy.wait_recv()
+    stage[...] = returned[...].reshape(stage.shape).astype(F32)
+    for b in range(blocks):
+        weighted[b * LANES:(b + 1) * LANES, :] = stage[pl.ds(b, reals, stride=blocks), :].T.astype(BF16)
+
+    span = rows * n_cell
+
+    def product(t):
+        at = pl.ds(pl.multiple_of(t * span, span), span)
+        return jnp.dot(picked[at, :], weighted[...], preferred_element_type=F32)
+
+    dp_copies, dx_copies, dc_copies = {}, {}, {}
+    order = [*range(1, n_hi), 0]
+    for q in order:
+        core_out[q] = product(hi_at(q) * 2 + (1 - core)).astype(BF16)
+        dp_copies[q] = go(remote(core_out.at[q], core_in.at[q], dp, q, partner))
+    far = sorted(range(n_cell), key=lambda k: -min(k, n_cell - k))
+    for q in order:
+        summed = product(hi_at(q) * 2 + core)
+        dp_copies[q].wait_recv()
+        total[...] = (summed + core_in[q].astype(F32)).reshape(n_cell, rows, LANES)
+        if q:
+            for k in far:
+                c = cell_at(k)
+                x_out[q, c] = total[c].astype(BF16)
+                dx_copies[q, k] = go(remote(x_out.at[q, c], x_in.at[q, c], dx, q * n_cell + k, x_peer(q)))
+    for k in far:
+        c = cell_at(k)
+        block_sum = total[c]
+        for q in range(1, n_hi):
+            dx_copies[q, k].wait_recv()
+            block_sum += x_in[q, c].astype(F32)
+        if k:
+            cell_out[c] = block_sum.astype(BF16)
+            dc_copies[k] = go(remote(cell_out.at[c], cell_in.at[k], dc, k, (tm, c)))
+    result = block_sum
+    for k in range(1, n_cell):
+        dc_copies[k].wait_recv()
+        result += cell_in[k].astype(F32)
+    out_ref[...] = result
+
+    for copy in sent:
+        copy.wait_send()
+
+
+PLAN = (0, 3, 3, 1)
+
+
+def field_program(n_tm, n_cell, sensitivity, duals, time_cov, cell_coords, obs_time, obs_owner):
+    obs, _, cells = sensitivity.shape
+    rows, reals = duals.shape
+    n_hi = n_tm // 2
+    devices = n_tm * n_cell
+    blocks = cells // LANES
+    grid_rows = n_cell * cells // LANES
+    duos = grid_rows // 2
+    span = rows * n_cell
+    vmem = pl.BlockSpec(memory_space=pltpu.VMEM)
+
+    def pair(count):
+        return [pltpu.SemaphoreType.DMA((count,)), pltpu.SemaphoreType.DMA((count,))]
+
+    return pl.pallas_call(
+        functools.partial(field_kernel, (n_hi, n_cell)),
+        out_shape=jax.ShapeDtypeStruct((rows, reals), F32),
+        in_specs=[
+            pl.BlockSpec(memory_space=pl.ANY), vmem, pl.BlockSpec(memory_space=pltpu.SMEM), vmem, vmem, vmem,
+        ],
+        out_specs=vmem,
+        scratch_shapes=[
+            pltpu.VMEM((obs, cells), BF16),
+            pltpu.VMEM((devices, rows, reals), BF16),
+            pltpu.VMEM((n_cell, 2, cells), jnp.int32),
+            pltpu.VMEM((cells, obs), BF16),
+            pltpu.VMEM((obs, cells), BF16),
+            pltpu.VMEM((obs, LANES), F32),
+            pltpu.VMEM((1, obs), F32),
+            pltpu.VMEM((2 * grid_rows - 1, LANES, LANES), BF16),
+            pltpu.VMEM((n_cell, 2 * LANES, cells), BF16),
+            pltpu.VMEM((n_cell, cells, 2 * LANES), BF16),
+            pltpu.VMEM((n_cell, 1, cells), jnp.int32),
+            pltpu.VMEM((reals * blocks, LANES), F32),
+            pltpu.VMEM((devices, TILE, LANES), BF16),
+            pltpu.VMEM((devices, TILE, LANES), BF16),
+            pltpu.VMEM((n_cell, n_tm * TILE, LANES), F32),
+            pltpu.VMEM((n_cell, duos * TILE, cells), BF16),
+            pltpu.VMEM(((duos + 2 * PAD) * TILE, 2 * LANES), BF16),
+            pltpu.VMEM((duos * TILE, 2 * LANES), F32),
+            pltpu.VMEM((n_cell, n_tm * TILE, LANES), F32),
+            pltpu.VMEM((devices, TILE, LANES), BF16),
+            pltpu.VMEM((devices, TILE, LANES), BF16),
+            pltpu.VMEM((cells, reals), BF16),
+            pltpu.VMEM((n_hi, span, reals), BF16),
+            pltpu.VMEM((n_hi, span, reals), BF16),
+            pltpu.VMEM((n_hi, n_cell, rows, reals), BF16),
+            pltpu.VMEM((n_hi, n_cell, rows, reals), BF16),
+            pltpu.VMEM((n_cell, rows, reals), F32),
+            pltpu.VMEM((n_cell, rows, reals), BF16),
+            pltpu.VMEM((n_cell, rows, reals), BF16),
+            pltpu.SemaphoreType.DMA,
+            *pair(n_cell), *pair(n_cell), *pair(n_hi * n_cell), *pair(n_hi * n_cell),
+            *pair(devices), *pair(devices),
+            *pair(n_hi), *pair(n_hi * n_cell), *pair(n_cell),
+        ],
+        compiler_params=pltpu.CompilerParams(
+            collective_id=0, has_side_effects=True, vmem_limit_bytes=62 * 1024 * 1024
+        ),
+    )(
+        sensitivity.reshape(obs, cells), duals, time_cov, cell_coords,
+        obs_time.reshape(1, obs), obs_owner.reshape(1, obs),
+    )
+
+
+def per_device(n_tm, n_cell, sensitivity, duals, *rest):
+    cells = sensitivity.shape[2]
+    rows, reals = duals.shape
+    devices = n_tm * n_cell
+    per = reals // devices
+    fits = (
+        rows % TILE == 0 and reals == LANES and cells % LANES == 0 and reals % devices == 0
+        and per * (cells // LANES) == TILE and per * n_tm == TILE and (n_cell * cells) % (2 * LANES) == 0
+    )
+    program = field_program if fits else ring_program
+    return program(n_tm, n_cell, sensitivity, duals, *rest)
+
+
 def solution(mesh):
     in_specs = (P(None, "tm", "cell"), P(("tm", "cell"), None), P(), P(None, "cell"), P(), P())
     out_specs = P(("tm", "cell"), None)

time: 51.7 us -> 47.8 us (0.925)
  Pallas kernels: 50 us -> 46.2 us
    pallas_call x1, Pallas kernels: 50 us -> 46.2 us  [field_program(): pl.pallas_call(functools.partial(field_kernel, (n_hi, n_cell)), out_shape...]
where the time goes in v1:
time: 47.8 us; the launch traced here: 47.6 us
  Pallas kernels  46.2 us (97%)
  local copies, waits for them, and re-layouts  1.38 us (3%)
    pallas_call x1, Pallas kernels, field_program(): pl.pallas_call(functools.partial(field_kernel, (n_hi, n_cell)), out_shape...  46.2 us
    unnamed x1, local copies, waits for them, and re-layouts  1.38 us

profile of v1, /device:TPU:0, one launch (start us, length us, event | category | flops | bytes accessed | tf_op | source)
XLA Modules:
  0.0 47.6 jit_solution(1318254641383243251)
XLA Ops:
  0.0 46.2 %shard_map.64 = f32[64,128]{1,0:T(8,128)} custom-call(bf16[2048,512]{1,0:T(8,128)(2,1)} %bitcast.3, bf16[64,128]{1,0:T(8,128)(2,1)} %duals_ref.1, f32[4,4]{1,0:T(4,128)} %cov_ref.1, s32[2,512]{1,0:T(2,128)} %coords_ref.1, s32[1,2048]{1,0:T(1,128)} %bitcast.4, s32[1,2048]{1,0:T(1,128)} %bitcast.5), custom_call_target="tpu_custom_call" | custom-call | tf_op jit(solution)/shard_map/pallas_call | solution.py:629
  46.2 1.4 %copy.8 = f32[64,128]{1,0:T(8,128)} copy(f32[64,128]{1,0:T(8,128)} %shard_map.64) | data formatting | bytes 65536

commit v2 on v1

--- a/solution.py
+++ b/solution.py
@@ -343,15 +343,17 @@
 TILE = 16
 
 
-def field_kernel(cfg, sens_hbm, duals_ref, cov_ref, coords_ref, time_ref, owner_ref, out_ref, *s):
+def field_kernel(
+    cfg, sens_hbm, duals_hbm, cov_hbm, coords_hbm, time_hbm, owner_hbm, out_ref, *s
+):
     n_hi, n_cell = cfg
-    n_tm = 2 * n_hi
-    (sens, full, coords_all, mask_t, picked, own_b, ids, toeplitz, hot_t, hot, halves, stage, tiles, fields, mixed,
-     placed, grid, acc, back, outs, returned, weighted, core_out, core_in, x_out, x_in, total, cell_out, cell_in,
-     local_sem, *pairs) = s
-    co, ac, ax, ap, ea, eb, dp, dx, dc = zip(pairs[0::2], pairs[1::2])
+    n_tm, n_z = 2 * n_hi, n_cell // 2
+    (sens, duals_ref, cov_ref, coords_ref, time_ref, owner_ref, full, coords_all, mask_t, picked, own_b, ids,
+     toeplitz, hot_t, hot, halves, stage, tiles, fields, mixed, placed, grid, acc, back, outs, returned, weighted,
+     core_out, core_in, plane_out, plane_in, sums, z_out, z_in, local_sems, *pairs) = s
+    cz, cy, az, ap, ac, ea, eb, dp, dx, dz = zip(pairs[0::2], pairs[1::2])
     obs, cells = sens.shape
-    rows = duals_ref.shape[0]
+    rows, reals = duals_ref.shape
     blocks = cells // LANES
     grid_rows = n_cell * cells // LANES
     duos = grid_rows // 2
@@ -360,14 +362,10 @@
     tm = lax.axis_index("tm")
     cell = lax.axis_index("cell")
     hi, core = tm // 2, tm % 2
+    z, y = cell // 2, cell % 2
     partner = (hi * 2 + (1 - core), cell)
     me = tm * n_cell + cell
-
-    def hi_at(q):
-        return lax.rem(hi + q + n_hi, n_hi)
-
-    def x_peer(q):
-        return (hi_at(q) * 2 + core, cell)
+    plane = [(dx_, dy_) for dx_ in range(n_hi) for dy_ in range(2)]
 
     def cell_at(k):
         return lax.rem(cell + k + n_cell, n_cell)
@@ -375,33 +373,76 @@
     def tm_at(a):
         return lax.rem(tm + a + n_tm, n_tm)
 
-    load = pltpu.make_async_copy(sens_hbm, sens, local_sem)
-    load.start()
+    def z_at(k):
+        return lax.rem(z + k + n_z, n_z)
+
+    def tm_in(shift):
+        return lax.rem(hi + shift[0], n_hi) * 2 + core
+
+    def y_in(shift):
+        return lax.rem(y + shift[1], 2)
+
+    def z_peer(k):
+        return (tm, z_at(k) * 2 + y)
+
+    def plane_peer(shift):
+        return (tm_in(shift), z * 2 + y_in(shift))
 
     barrier = pltpu.get_barrier_semaphore()
-    peers = [(tm, cell_at(k)) for k in range(1, n_cell)] + [x_peer(q) for q in range(1, n_hi)] + [partner]
+    peers = [z_peer(k) for k in range(1, n_z)] + [plane_peer(shift) for shift in plane[1:]] + [partner]
     for peer in peers:
         pl.semaphore_signal(barrier, inc=1, device_id=peer, device_id_type=MESH)
+
+    loads = [
+        pltpu.make_async_copy(src, dst, local_sems.at[i])
+        for i, (src, dst) in enumerate([
+            (duals_hbm, duals_ref), (coords_hbm, coords_ref), (time_hbm, time_ref), (owner_hbm, owner_ref),
+            (cov_hbm, cov_ref), (sens_hbm, sens),
+        ])
+    ]
+    for load in loads:
+        load.start()
+    loads[0].wait()
+    loads[1].wait()
+    pl.semaphore_wait(barrier, len(peers))
+
+    sent = []
+
+    def go(copy):
+        copy.start()
+        sent.append(copy)
+        return copy
+
+    def block_of(shift, k):
+        return full.at[tm_in(shift) * n_cell + z_at(-k) * 2 + y_in(shift)]
+
+    az_copies, ap_copies, ac_copies, cz_copies, cy_copies = {}, {}, {}, {}, {}
+
+    def forward_plane(src, k):
+        for j, shift in enumerate(plane):
+            if j:
+                ap_copies[j, k] = go(remote(src, block_of((0, 0), k), ap, j * n_z + k, plane_peer(shift)))
+
+    def forward_core(src, j, k):
+        ac_copies[j, k] = go(remote(src, block_of(plane[j], k), ac, j * n_z + k, partner))
+
+    for k in range(1, n_z):
+        az_copies[k] = go(remote(duals_ref, block_of((0, 0), 0), az, k, z_peer(k)))
+    forward_plane(duals_ref, 0)
+    forward_core(duals_ref, 0, 0)
+    for k in range(1, n_z):
+        cz_copies[k] = go(remote(coords_ref, coords_all.at[cell], cz, k, z_peer(k)))
+    cy_copies[0] = go(remote(coords_ref, coords_all.at[cell], cy, 0, plane_peer((0, 1))))
+    full[me] = duals_ref[...]
     coords_all[cell] = coords_ref[...]
+
+    loads[2].wait()
+    loads[3].wait()
     own_b[...] = column_of(owner_ref[...].astype(F32))
     live = tm <= time_ref[...]
     ids[...] = jnp.where(live, lax.broadcasted_iota(jnp.int32, (1, obs), 1), -1).astype(F32)
-
-    col_gap = (
-        lax.broadcasted_iota(jnp.int32, (LANES, LANES), 0) - lax.broadcasted_iota(jnp.int32, (LANES, LANES), 1)
-    ).astype(F32)
-    col_gap = col_gap * col_gap
-    grid[...] = jnp.zeros_like(grid)
-
-    @pl.loop(0, grid_rows)
-    def _(gap):
-        row_gap = gap.astype(F32)
-        distance = jnp.sqrt(row_gap * row_gap + col_gap)
-        block = (jnp.exp(-distance / LSCALE) / (8.0 * LSCALE)).astype(BF16)
-        toeplitz[grid_rows - 1 - gap] = block
-        toeplitz[grid_rows - 1 + gap] = block
-
-    load.wait()
+    loads[4].wait()
+    loads[5].wait()
 
     @pl.loop(0, obs // PICK_ROWS)
     def _(i):
@@ -428,52 +469,40 @@
                 fillers.pop(0)()
 
     fill(PLAN[0])
-    pl.semaphore_wait(barrier, len(peers))
-
-    sent = []
-
-    def go(copy):
-        copy.start()
-        sent.append(copy)
-        return copy
-
-    def block_of(t, c):
-        return full.at[t * n_cell + c]
-
-    co_copies, cell_copies, x_copies, core_copies = {}, {}, {}, {}
-
-    def forward_x(src, k):
-        for q in range(1, n_hi):
-            x_copies[q, k] = go(remote(src, block_of(tm, cell_at(-k)), ax, q * n_cell + k, x_peer(q)))
-
-    def forward_core(src, q, k):
-        dst = block_of(hi_at(-q) * 2 + core, cell_at(-k))
-        core_copies[q, k] = go(remote(src, dst, ap, q * n_cell + k, partner))
-
-    for k in range(1, n_cell):
-        cell_copies[k] = go(remote(duals_ref, block_of(tm, cell), ac, k, (tm, cell_at(k))))
-    forward_x(duals_ref, 0)
-    forward_core(duals_ref, 0, 0)
-    for k in range(1, n_cell):
-        co_copies[k] = go(remote(coords_ref, coords_all.at[cell], co, k, (tm, cell_at(k))))
-    full[me] = duals_ref[...]
+    for k in range(1, n_z):
+        az_copies[k].wait_recv()
+        src = block_of((0, 0), k)
+        forward_plane(src, k)
+        forward_core(src, 0, k)
+    for k in range(1, n_z):
+        cz_copies[k].wait_recv()
+        got = coords_all.at[z_at(-k) * 2 + y]
+        cy_copies[k] = go(remote(got, got, cy, k, plane_peer((0, 1))))
+
+    col_gap = (
+        lax.broadcasted_iota(jnp.int32, (LANES, LANES), 0) - lax.broadcasted_iota(jnp.int32, (LANES, LANES), 1)
+    ).astype(F32)
+    col_gap = col_gap * col_gap
+    grid[...] = jnp.zeros_like(grid)
+
+    @pl.loop(0, grid_rows)
+    def _(gap):
+        row_gap = gap.astype(F32)
+        distance = jnp.sqrt(row_gap * row_gap + col_gap)
+        block = (jnp.exp(-distance / LSCALE) / (8.0 * LSCALE)).astype(BF16)
+        toeplitz[grid_rows - 1 - gap] = block
+        toeplitz[grid_rows - 1 + gap] = block
 
     fill(PLAN[1])
-    for k in range(1, n_cell):
-        cell_copies[k].wait_recv()
-        src = block_of(tm, cell_at(-k))
-        forward_x(src, k)
-        forward_core(src, 0, k)
+    for k in range(n_z):
+        for j in range(1, len(plane)):
+            ap_copies[j, k].wait_recv()
+            forward_core(block_of(plane[j], k), j, k)
     fill(PLAN[2])
-    for k in range(n_cell):
-        for q in range(1, n_hi):
-            x_copies[q, k].wait_recv()
-            forward_core(block_of(hi_at(-q) * 2 + core, cell_at(-k)), q, k)
-    for k in range(n_cell):
-        for q in range(n_hi):
-            core_copies[q, k].wait_recv()
-
-    reals = duals_ref.shape[1]
+    for k in range(n_z):
+        for j in range(len(plane)):
+            ac_copies[j, k].wait_recv()
+
     adjoint = jnp.dot(mask_t[...], full[...].reshape(obs, reals), preferred_element_type=F32)
     for b in range(blocks):
         stage[pl.ds(b, reals, stride=blocks), :] = adjoint[b * LANES:(b + 1) * LANES, :].T
@@ -489,8 +518,8 @@
             )
     fields[me] = tiles[me]
 
-    for k in range(1, n_cell):
-        co_copies[k].wait_recv()
+    for k in range(n_z):
+        cy_copies[k].wait_recv()
     for k in range(n_cell):
         code = (coords_all[k, 0:1, :] & 1) * LANES + coords_all[k, 1:2, :]
         spots = lax.broadcasted_iota(jnp.int32, (wide, cells), 0)
@@ -569,47 +598,61 @@
     for b in range(blocks):
         weighted[b * LANES:(b + 1) * LANES, :] = stage[pl.ds(b, reals, stride=blocks), :].T.astype(BF16)
 
-    span = rows * n_cell
-
-    def product(t):
-        at = pl.ds(pl.multiple_of(t * span, span), span)
-        return jnp.dot(picked[at, :], weighted[...], preferred_element_type=F32)
-
-    dp_copies, dx_copies, dc_copies = {}, {}, {}
-    order = [*range(1, n_hi), 0]
-    for q in order:
-        core_out[q] = product(hi_at(q) * 2 + (1 - core)).astype(BF16)
-        dp_copies[q] = go(remote(core_out.at[q], core_in.at[q], dp, q, partner))
-    far = sorted(range(n_cell), key=lambda k: -min(k, n_cell - k))
-    for q in order:
-        summed = product(hi_at(q) * 2 + core)
-        dp_copies[q].wait_recv()
-        total[...] = (summed + core_in[q].astype(F32)).reshape(n_cell, rows, LANES)
-        if q:
-            for k in far:
-                c = cell_at(k)
-                x_out[q, c] = total[c].astype(BF16)
-                dx_copies[q, k] = go(remote(x_out.at[q, c], x_in.at[q, c], dx, q * n_cell + k, x_peer(q)))
-    for k in far:
-        c = cell_at(k)
-        block_sum = total[c]
-        for q in range(1, n_hi):
-            dx_copies[q, k].wait_recv()
-            block_sum += x_in[q, c].astype(F32)
-        if k:
-            cell_out[c] = block_sum.astype(BF16)
-            dc_copies[k] = go(remote(cell_out.at[c], cell_in.at[k], dc, k, (tm, c)))
-    result = block_sum
-    for k in range(1, n_cell):
-        dc_copies[k].wait_recv()
-        result += cell_in[k].astype(F32)
+    deep = 2 * rows
+
+    def product(t, d):
+        at = pl.ds(pl.multiple_of((t * n_cell + 2 * d) * rows, deep), deep)
+        return jnp.dot(picked[at, :], weighted[...], preferred_element_type=F32).reshape(2, rows, reals)
+
+    dp_copies, dx_copies = {}, {}
+    for d in range(n_z):
+        for h in range(n_hi):
+            core_out[d, h] = product(h * 2 + (1 - core), d).astype(BF16)
+        dp_copies[d] = go(remote(core_out.at[d], core_in.at[d], dp, d, partner))
+    for d in range(n_z):
+        terms = [product(h * 2 + core, d) for h in range(n_hi)]
+        dp_copies[d].wait_recv()
+        for h in range(n_hi):
+            total = terms[h] + core_in[d, h].astype(F32)
+            plane_out[d, h] = total.astype(BF16)
+            sums[d, h] = total
+        for j, shift in enumerate(plane):
+            if j:
+                src = plane_out.at[d, lax.rem(hi + shift[0], n_hi), y_in(shift)]
+                dx_copies[j, d] = go(
+                    remote(src, plane_in.at[d, j], dx, j * n_z + d, plane_peer(shift))
+                )
+
+    def z_copy(d, at):
+        return remote(z_out.at[d], z_in.at[at], dz, at, (tm, d * 2 + y))
+
+    for d in range(n_z):
+        part = sums[d, hi, y]
+        for j in range(1, len(plane)):
+            dx_copies[j, d].wait_recv()
+            part += plane_in[d, j].astype(F32)
+        sums[d, 0, 0] = part
+        z_out[d] = part.astype(BF16)
+
+        @pl.when(z != d)
+        def _():
+            z_copy(d, z).start()
+
+    result = sums[z, 0, 0]
+    for k in range(1, n_z):
+        z_copy(z_at(k), z_at(k)).wait_recv()
+        result += z_in[z_at(k)].astype(F32)
     out_ref[...] = result
 
     for copy in sent:
         copy.wait_send()
-
-
-PLAN = (0, 3, 3, 1)
+    for d in range(n_z):
+        @pl.when(z != d)
+        def _():
+            z_copy(d, z).wait_send()
+
+
+PLAN = (1, 3, 2, 1)
 
 
 def field_program(n_tm, n_cell, sensitivity, duals, time_cov, cell_coords, obs_time, obs_owner):
@@ -620,8 +663,7 @@
     blocks = cells // LANES
     grid_rows = n_cell * cells // LANES
     duos = grid_rows // 2
-    span = rows * n_cell
-    vmem = pl.BlockSpec(memory_space=pltpu.VMEM)
+    n_z = n_cell // 2
 
     def pair(count):
         return [pltpu.SemaphoreType.DMA((count,)), pltpu.SemaphoreType.DMA((count,))]
@@ -629,12 +671,15 @@
     return pl.pallas_call(
         functools.partial(field_kernel, (n_hi, n_cell)),
         out_shape=jax.ShapeDtypeStruct((rows, reals), F32),
-        in_specs=[
-            pl.BlockSpec(memory_space=pl.ANY), vmem, pl.BlockSpec(memory_space=pltpu.SMEM), vmem, vmem, vmem,
-        ],
-        out_specs=vmem,
+        in_specs=[pl.BlockSpec(memory_space=pl.ANY)] * 6,
+        out_specs=pl.BlockSpec(memory_space=pltpu.VMEM),
         scratch_shapes=[
             pltpu.VMEM((obs, cells), BF16),
+            pltpu.VMEM((rows, reals), BF16),
+            pltpu.SMEM((n_tm, n_tm), F32),
+            pltpu.VMEM((2, cells), jnp.int32),
+            pltpu.VMEM((1, obs), jnp.int32),
+            pltpu.VMEM((1, obs), jnp.int32),
             pltpu.VMEM((devices, rows, reals), BF16),
             pltpu.VMEM((n_cell, 2, cells), jnp.int32),
             pltpu.VMEM((cells, obs), BF16),
@@ -656,17 +701,17 @@
             pltpu.VMEM((devices, TILE, LANES), BF16),
             pltpu.VMEM((devices, TILE, LANES), BF16),
             pltpu.VMEM((cells, reals), BF16),
-            pltpu.VMEM((n_hi, span, reals), BF16),
-            pltpu.VMEM((n_hi, span, reals), BF16),
-            pltpu.VMEM((n_hi, n_cell, rows, reals), BF16),
-            pltpu.VMEM((n_hi, n_cell, rows, reals), BF16),
-            pltpu.VMEM((n_cell, rows, reals), F32),
-            pltpu.VMEM((n_cell, rows, reals), BF16),
-            pltpu.VMEM((n_cell, rows, reals), BF16),
-            pltpu.SemaphoreType.DMA,
-            *pair(n_cell), *pair(n_cell), *pair(n_hi * n_cell), *pair(n_hi * n_cell),
+            pltpu.VMEM((n_z, n_hi, 2, rows, reals), BF16),
+            pltpu.VMEM((n_z, n_hi, 2, rows, reals), BF16),
+            pltpu.VMEM((n_z, n_hi, 2, rows, reals), BF16),
+            pltpu.VMEM((n_z, 2 * n_hi, rows, reals), BF16),
+            pltpu.VMEM((n_z, n_hi, 2, rows, reals), F32),
+            pltpu.VMEM((n_z, rows, reals), BF16),
+            pltpu.VMEM((n_z, rows, reals), BF16),
+            pltpu.SemaphoreType.DMA((6,)),
+            *pair(n_z), *pair(n_z), *pair(n_z), *pair(2 * n_hi * n_z), *pair(2 * n_hi * n_z),
             *pair(devices), *pair(devices),
-            *pair(n_hi), *pair(n_hi * n_cell), *pair(n_cell),
+            *pair(n_z), *pair(2 * n_hi * n_z), *pair(n_z),
         ],
         compiler_params=pltpu.CompilerParams(
             collective_id=0, has_side_effects=True, vmem_limit_bytes=62 * 1024 * 1024
@@ -683,7 +728,7 @@
     devices = n_tm * n_cell
     per = reals // devices
     fits = (
-        rows % TILE == 0 and reals == LANES and cells % LANES == 0 and reals % devices == 0
+        n_tm == 4 and n_cell % 2 == 0 and rows % TILE == 0 and reals == LANES and cells % LANES == 0 and reals % devices == 0
         and per * (cells // LANES) == TILE and per * n_tm == TILE and (n_cell * cells) % (2 * LANES) == 0
     )
     program = field_program if fits else ring_program

time: 47.8 us -> 44.4 us (0.929)
  Pallas kernels: 46.2 us -> 42.8 us
    pallas_call x1, Pallas kernels: 46.2 us -> 42.8 us  [field_program(): pl.pallas_call(functools.partial(field_kernel, (n_hi, n_cell)), out_shape...]
where the time goes in v2:
time: 44.4 us; the launch traced here: 44.2 us
  Pallas kernels  42.8 us (96%)
  local copies, waits for them, and re-layouts  1.38 us (3%)
    pallas_call x1, Pallas kernels, field_program(): pl.pallas_call(functools.partial(field_kernel, (n_hi, n_cell)), out_shape...  42.8 us
    unnamed x1, local copies, waits for them, and re-layouts  1.38 us

profile of v2, /device:TPU:0, one launch (start us, length us, event | category | flops | bytes accessed | tf_op | source)
XLA Modules:
  0.0 44.2 jit_solution(13265357616120330668)
XLA Ops:
  0.0 42.8 %shard_map.64 = f32[64,128]{1,0:T(8,128)} custom-call(bf16[2048,512]{1,0:T(8,128)(2,1)} %bitcast.3, bf16[64,128]{1,0:T(8,128)(2,1)} %duals_hbm.1, f32[4,4]{1,0:T(4,128)} %cov_hbm.1, s32[2,512]{1,0:T(2,128)} %coords_hbm.1, s32[1,2048]{1,0:T(1,128)} %bitcast.4, s32[1,2048]{1,0:T(1,128)} %bitcast.5), custom_call_target="tpu_custom_call" | custom-call | tf_op jit(solution)/shard_map/pallas_call | solution.py:671
  42.8 1.4 %copy.8 = f32[64,128]{1,0:T(8,128)} copy(f32[64,128]{1,0:T(8,128)} %shard_map.64) | data formatting | bytes 65536

commit v3 on v2

--- a/solution.py
+++ b/solution.py
@@ -479,20 +479,6 @@
         got = coords_all.at[z_at(-k) * 2 + y]
         cy_copies[k] = go(remote(got, got, cy, k, plane_peer((0, 1))))
 
-    col_gap = (
-        lax.broadcasted_iota(jnp.int32, (LANES, LANES), 0) - lax.broadcasted_iota(jnp.int32, (LANES, LANES), 1)
-    ).astype(F32)
-    col_gap = col_gap * col_gap
-    grid[...] = jnp.zeros_like(grid)
-
-    @pl.loop(0, grid_rows)
-    def _(gap):
-        row_gap = gap.astype(F32)
-        distance = jnp.sqrt(row_gap * row_gap + col_gap)
-        block = (jnp.exp(-distance / LSCALE) / (8.0 * LSCALE)).astype(BF16)
-        toeplitz[grid_rows - 1 - gap] = block
-        toeplitz[grid_rows - 1 + gap] = block
-
     fill(PLAN[1])
     for k in range(n_z):
         for j in range(1, len(plane)):
@@ -527,6 +513,20 @@
         hot_t[k] = ones
         hot[k] = ones.T
         halves[k] = coords_all[k, 0:1, :] >> 1
+    col_gap = (
+        lax.broadcasted_iota(jnp.int32, (LANES, LANES), 0) - lax.broadcasted_iota(jnp.int32, (LANES, LANES), 1)
+    ).astype(F32)
+    col_gap = col_gap * col_gap
+    grid[...] = jnp.zeros_like(grid)
+
+    @pl.loop(0, grid_rows)
+    def _(gap):
+        row_gap = gap.astype(F32)
+        distance = jnp.sqrt(row_gap * row_gap + col_gap)
+        block = (jnp.exp(-distance / LSCALE) / (8.0 * LSCALE)).astype(BF16)
+        toeplitz[grid_rows - 1 - gap] = block
+        toeplitz[grid_rows - 1 + gap] = block
+
     fill(PLAN[3])
 
     for copy in ea_copies.values():
@@ -616,6 +616,12 @@
             total = terms[h] + core_in[d, h].astype(F32)
             plane_out[d, h] = total.astype(BF16)
             sums[d, h] = total
+        if d == 1:
+            @pl.when(core == 1)
+            def _():
+                for j in (1,):
+                    dx_copies[j, 0].wait_recv()
+
         for j, shift in enumerate(plane):
             if j:
                 src = plane_out.at[d, lax.rem(hi + shift[0], n_hi), y_in(shift)]
@@ -628,8 +634,15 @@
 
     for d in range(n_z):
         part = sums[d, hi, y]
+        if d == 0:
+            @pl.when(core == 0)
+            def _():
+                for j in (1,):
+                    dx_copies[j, d].wait_recv()
+
         for j in range(1, len(plane)):
-            dx_copies[j, d].wait_recv()
+            if d != 0 or j not in (1,):
+                dx_copies[j, d].wait_recv()
             part += plane_in[d, j].astype(F32)
         sums[d, 0, 0] = part
         z_out[d] = part.astype(BF16)
@@ -652,7 +665,7 @@
             z_copy(d, z).wait_send()
 
 
-PLAN = (1, 3, 2, 1)
+PLAN = (0, 0, 0, 2)
 
 
 def field_program(n_tm, n_cell, sensitivity, duals, time_cov, cell_coords, obs_time, obs_owner):

time: 44.4 us -> 42.4 us (0.955)
  Pallas kernels: 42.8 us -> 40.8 us
    pallas_call x1, Pallas kernels: 42.8 us -> 40.8 us  [field_program(): pl.pallas_call(functools.partial(field_kernel, (n_hi, n_cell)), out_shape...]
where the time goes in v3:
time: 42.4 us; the launch traced here: 42.2 us
  Pallas kernels  40.8 us (96%)
  local copies, waits for them, and re-layouts  1.38 us (3%)
    pallas_call x1, Pallas kernels, field_program(): pl.pallas_call(functools.partial(field_kernel, (n_hi, n_cell)), out_shape...  40.8 us
    unnamed x1, local copies, waits for them, and re-layouts  1.38 us

profile of v3, /device:TPU:0, one launch (start us, length us, event | category | flops | bytes accessed | tf_op | source)
XLA Modules:
  0.0 42.2 jit_solution(1888657855867990207)
XLA Ops:
  0.0 40.8 %shard_map.64 = f32[64,128]{1,0:T(8,128)} custom-call(bf16[2048,512]{1,0:T(8,128)(2,1)} %bitcast.3, bf16[64,128]{1,0:T(8,128)(2,1)} %duals_hbm.1, f32[4,4]{1,0:T(4,128)} %cov_hbm.1, s32[2,512]{1,0:T(2,128)} %coords_hbm.1, s32[1,2048]{1,0:T(1,128)} %bitcast.4, s32[1,2048]{1,0:T(1,128)} %bitcast.5), custom_call_target="tpu_custom_call" | custom-call | tf_op jit(solution)/shard_map/pallas_call | solution.py:684
  40.8 1.4 %copy.8 = f32[64,128]{1,0:T(8,128)} copy(f32[64,128]{1,0:T(8,128)} %shard_map.64) | data formatting | bytes 65536

commit v4 on v3

--- a/solution.py
+++ b/solution.py
@@ -349,7 +349,7 @@
     n_hi, n_cell = cfg
     n_tm, n_z = 2 * n_hi, n_cell // 2
     (sens, duals_ref, cov_ref, coords_ref, time_ref, owner_ref, full, coords_all, mask_t, picked, own_b, ids,
-     toeplitz, hot_t, hot, halves, stage, tiles, fields, mixed, placed, grid, acc, back, outs, returned, weighted,
+     toeplitz, hot_t, hot, halves, row_hot, stage, tiles, fields, mixed, grid, acc, back, outs, returned, weighted,
      core_out, core_in, plane_out, plane_in, sums, z_out, z_in, local_sems, *pairs) = s
     cz, cy, az, ap, ac, ea, eb, dp, dx, dz = zip(pairs[0::2], pairs[1::2])
     obs, cells = sens.shape
@@ -367,12 +367,6 @@
     me = tm * n_cell + cell
     plane = [(dx_, dy_) for dx_ in range(n_hi) for dy_ in range(2)]
 
-    def cell_at(k):
-        return lax.rem(cell + k + n_cell, n_cell)
-
-    def tm_at(a):
-        return lax.rem(tm + a + n_tm, n_tm)
-
     def z_at(k):
         return lax.rem(z + k + n_z, n_z)
 
@@ -387,6 +381,27 @@
 
     def plane_peer(shift):
         return (tm_in(shift), z * 2 + y_in(shift))
+
+    def far_z(i):
+        skew = jnp.where(2 * z < n_z - 1, n_z - 1 - 2 * z, 2 * z - (n_z - 1))
+        reach = jnp.where(2 * z < n_z - 1, z, n_z - 1 - z)
+        aside = jnp.where(2 * z < n_z - 1, n_z - 1 - i, i)
+        turn = jnp.where(i < skew, 0, i - skew)
+        gap = reach - turn // 2
+        return jnp.where(i < skew, aside, z + jnp.where(turn % 2 == 0, gap, -gap))
+
+    far_cells = [far_z(i) * 2 + lax.rem(y + f, 2) for i in range(n_z) for f in (1, 0)]
+    shifts = [(fx, fc) for fx in (1, 0) for fc in (1, 0)]
+
+    def tm_flip(shift):
+        return lax.rem(hi + shift[0], n_hi) * 2 + lax.rem(core + shift[1], 2)
+
+    def swap(src, dst, sems, there, here, device):
+        send, recv = sems
+        return pltpu.make_async_remote_copy(
+            src_ref=src, dst_ref=dst, send_sem=send.at[there], recv_sem=recv.at[here],
+            device_id=device, device_id_type=MESH,
+        )
 
     barrier = pltpu.get_barrier_semaphore()
     peers = [z_peer(k) for k in range(1, n_z)] + [plane_peer(shift) for shift in plane[1:]] + [partner]
@@ -494,14 +509,13 @@
         stage[pl.ds(b, reals, stride=blocks), :] = adjoint[b * LANES:(b + 1) * LANES, :].T
     tiles[...] = stage[...].astype(BF16).reshape(tiles.shape)
 
-    shifts = [(a, k) for k in sorted(range(n_cell), key=lambda k: -min(k, n_cell - k)) for a in range(n_tm)]
-    ea_copies = {}
-    for a, k in shifts:
-        if (a, k) != (0, 0):
-            peer = (tm_at(a), cell_at(k))
-            ea_copies[a, k] = go(
-                remote(tiles.at[peer[0] * n_cell + peer[1]], fields.at[me], ea, a * n_cell + k, peer)
-            )
+    last = len(far_cells) - 1
+    for i, c in enumerate(far_cells):
+        for shift in shifts:
+            if i < last or shift != (0, 0):
+                t = tm_flip(shift)
+                there = t * n_cell + c
+                go(swap(tiles.at[there], fields.at[me], ea, there, me, (t, c)))
     fields[me] = tiles[me]
 
     for k in range(n_z):
@@ -513,6 +527,8 @@
         hot_t[k] = ones
         hot[k] = ones.T
         halves[k] = coords_all[k, 0:1, :] >> 1
+        duo = lax.broadcasted_iota(jnp.int32, (duos * TILE, cells), 0) // TILE
+        row_hot[k] = jnp.where(duo == halves[k], 1.0, 0.0).astype(BF16)
     col_gap = (
         lax.broadcasted_iota(jnp.int32, (LANES, LANES), 0) - lax.broadcasted_iota(jnp.int32, (LANES, LANES), 1)
     ).astype(F32)
@@ -529,23 +545,28 @@
 
     fill(PLAN[3])
 
-    for copy in ea_copies.values():
-        copy.wait_recv()
-    for k in range(n_cell):
-        got = [fields[t * n_cell + k].astype(F32) for t in range(n_tm)]
+    for i, c in reversed(list(enumerate(far_cells))):
+        for shift in reversed(shifts):
+            if i < last or shift != (0, 0):
+                t = tm_flip(shift)
+                there = t * n_cell + c
+                swap(tiles.at[me], fields.at[there], ea, there, there, (t, c)).wait_recv()
+        got = [fields[t * n_cell + c].astype(F32) for t in range(n_tm)]
         for t in range(n_tm):
             blend = cov_ref[t, 0] * got[0]
             for u in range(1, n_tm):
                 blend += cov_ref[t, u] * got[u]
-            mixed[k, t * TILE:(t + 1) * TILE, :] = blend
-        for b in range(blocks):
-            lanes = slice(b * LANES, (b + 1) * LANES)
-            x = mixed[k, pl.ds(b, TILE, stride=blocks), :]
-            for d in range(duos):
-                placed[k, d * TILE:(d + 1) * TILE, lanes] = jnp.where(halves[k, 0:1, lanes] == d, x, 0.0).astype(BF16)
-    on_grid = jnp.dot(placed[0], hot[0], preferred_element_type=F32)
-    for k in range(1, n_cell):
-        on_grid += jnp.dot(placed[k], hot[k], preferred_element_type=F32)
+            mixed[i, t * TILE:(t + 1) * TILE, :] = blend
+        x = jnp.concatenate(
+            [mixed[i, pl.ds(b, TILE, stride=blocks), :].astype(BF16) for b in range(blocks)], axis=1
+        )
+        placed = (row_hot[c].reshape(duos, TILE, cells) * x[None]).reshape(duos * TILE, cells)
+        term = jnp.dot(placed, hot[c], preferred_element_type=F32)
+        if i == last:
+            acc[...] = term
+        else:
+            acc[...] += term
+    on_grid = acc[...]
     grid[PAD * TILE:(PAD + duos) * TILE, :] = on_grid.astype(BF16)
 
     def covariance(m):
@@ -571,9 +592,7 @@
             acc[at, :] += term
 
     smooth = acc[...].astype(BF16)
-    eb_copies = {}
-    for k in sorted(range(n_cell), key=lambda k: -min(k, n_cell - k)):
-        c = cell_at(k)
+    for i, c in enumerate(far_cells):
         spread = jnp.dot(smooth, hot_t[c], preferred_element_type=F32)
         for b in range(blocks):
             lanes = slice(b * LANES, (b + 1) * LANES)
@@ -581,19 +600,22 @@
             found = spread[0:TILE, lanes]
             for d in range(1, duos):
                 found = jnp.where(half == d, spread[d * TILE:(d + 1) * TILE, lanes], found)
-            back[k, pl.ds(b, TILE, stride=blocks), :] = found
+            back[i, pl.ds(b, TILE, stride=blocks), :] = found
         for t in range(n_tm):
-            outs[t * n_cell + c] = back[k, t * TILE:(t + 1) * TILE, :].astype(BF16)
-        for a in range(n_tm):
-            if (a, k) != (0, 0):
-                peer = (tm_at(a), c)
-                eb_copies[a, k] = go(
-                    remote(outs.at[peer[0] * n_cell + c], returned.at[me], eb, a * n_cell + k, peer)
-                )
+            outs[t * n_cell + c] = back[i, t * TILE:(t + 1) * TILE, :].astype(BF16)
+        for shift in shifts:
+            if i < last or shift != (0, 0):
+                t = tm_flip(shift)
+                there = t * n_cell + c
+                go(swap(outs.at[there], returned.at[me], eb, there, me, (t, c)))
     returned[me] = outs[me]
     fill(len(fillers))
-    for copy in eb_copies.values():
-        copy.wait_recv()
+    for i, c in reversed(list(enumerate(far_cells))):
+        for shift in shifts:
+            if i < last or shift != (0, 0):
+                t = tm_flip(shift)
+                there = t * n_cell + c
+                swap(outs.at[me], returned.at[there], eb, there, there, (t, c)).wait_recv()
     stage[...] = returned[...].reshape(stage.shape).astype(F32)
     for b in range(blocks):
         weighted[b * LANES:(b + 1) * LANES, :] = stage[pl.ds(b, reals, stride=blocks), :].T.astype(BF16)
@@ -665,7 +687,7 @@
             z_copy(d, z).wait_send()
 
 
-PLAN = (0, 0, 0, 2)
+PLAN = (0, 1, 0, 1)
 
 
 def field_program(n_tm, n_cell, sensitivity, duals, time_cov, cell_coords, obs_time, obs_owner):
@@ -684,7 +706,7 @@
     return pl.pallas_call(
         functools.partial(field_kernel, (n_hi, n_cell)),
         out_shape=jax.ShapeDtypeStruct((rows, reals), F32),
-        in_specs=[pl.BlockSpec(memory_space=pl.ANY)] * 6,
+        in_specs=[pl.BlockSpec(memory_space=pltpu.HBM)] * 6,
         out_specs=pl.BlockSpec(memory_space=pltpu.VMEM),
         scratch_shapes=[
             pltpu.VMEM((obs, cells), BF16),
@@ -703,11 +725,11 @@
             pltpu.VMEM((n_cell, 2 * LANES, cells), BF16),
             pltpu.VMEM((n_cell, cells, 2 * LANES), BF16),
             pltpu.VMEM((n_cell, 1, cells), jnp.int32),
+            pltpu.VMEM((n_cell, duos * TILE, cells), BF16),
             pltpu.VMEM((reals * blocks, LANES), F32),
             pltpu.VMEM((devices, TILE, LANES), BF16),
             pltpu.VMEM((devices, TILE, LANES), BF16),
             pltpu.VMEM((n_cell, n_tm * TILE, LANES), F32),
-            pltpu.VMEM((n_cell, duos * TILE, cells), BF16),
             pltpu.VMEM(((duos + 2 * PAD) * TILE, 2 * LANES), BF16),
             pltpu.VMEM((duos * TILE, 2 * LANES), F32),
             pltpu.VMEM((n_cell, n_tm * TILE, LANES), F32),
@@ -727,12 +749,14 @@
             *pair(n_z), *pair(2 * n_hi * n_z), *pair(n_z),
         ],
         compiler_params=pltpu.CompilerParams(
-            collective_id=0, has_side_effects=True, vmem_limit_bytes=62 * 1024 * 1024
+            collective_id=0, has_side_effects=True, vmem_limit_bytes=40 * 1024 * 1024
         ),
-    )(
-        sensitivity.reshape(obs, cells), duals, time_cov, cell_coords,
-        obs_time.reshape(1, obs), obs_owner.reshape(1, obs),
-    )
+    )(*[
+        pltpu.with_memory_space_constraint(x, pltpu.HBM) for x in (
+            sensitivity.reshape(obs, cells), duals, time_cov, cell_coords,
+            obs_time.reshape(1, obs), obs_owner.reshape(1, obs),
+        )
+    ])
 
 
 def per_device(n_tm, n_cell, sensitivity, duals, *rest):

time: 42.4 us -> 39.7 us (0.936)
  Pallas kernels: 40.8 us -> 38.9 us
  local copies, waits for them, and re-layouts: 1.38 us -> 0.62 us
    pallas_call x1, Pallas kernels: 40.8 us -> 38.9 us  [field_program(): pl.pallas_call(functools.partial(field_kernel, (n_hi, n_cell)), out_shape...]
    unnamed x1, local copies, waits for them, and re-layouts: 1.38 us -> 0.62 us
where the time goes in v4:
time: 39.7 us; the launch traced here: 39.5 us
  Pallas kernels  38.9 us (98%)
  local copies, waits for them, and re-layouts  0.62 us (2%)
    pallas_call x1, Pallas kernels, field_program(): pl.pallas_call(functools.partial(field_kernel, (n_hi, n_cell)), out_shape...  38.9 us

profile of v4, /device:TPU:0, one launch (start us, length us, event | category | flops | bytes accessed | tf_op | source)
XLA Modules:
  0.0 39.5 jit_solution(9951965199894088388)
XLA Ops:
  0.0 38.9 %shard_map.64 = f32[64,128]{1,0:T(8,128)S(1)} custom-call(bf16[2048,512]{1,0:T(8,128)(2,1)} %bitcast.3, bf16[64,128]{1,0:T(8,128)(2,1)} %duals_hbm.1, f32[4,4]{1,0:T(4,128)} %cov_hbm.1, s32[2,512]{1,0:T(2,128)} %coords_hbm.1, s32[1,2048]{1,0:T(1,128)} %bitcast.4, s32[1,2048]{1,0:T(1,128)} %bitcast.5), custom_call_target="tpu_custom_call" | custom-call | tf_op jit(solution)/shard_map/pallas_call | solution.py:706
  38.9 0.6 %copy.8 = f32[64,128]{1,0:T(8,128)} copy(f32[64,128]{1,0:T(8,128)S(1)} %shard_map.64) | data formatting | bytes 65536

commit v5 on v4

--- a/solution.py
+++ b/solution.py
@@ -404,7 +404,7 @@
         )
 
     barrier = pltpu.get_barrier_semaphore()
-    peers = [z_peer(k) for k in range(1, n_z)] + [plane_peer(shift) for shift in plane[1:]] + [partner]
+    peers = [z_peer(k) for k in range(1, n_z)] + [plane_peer(shift) for shift in plane[1:3]] + [partner]
     for peer in peers:
         pl.semaphore_signal(barrier, inc=1, device_id=peer, device_id_type=MESH)
 
@@ -419,6 +419,20 @@
         load.start()
     loads[0].wait()
     loads[1].wait()
+    col_gap = (
+        lax.broadcasted_iota(jnp.int32, (LANES, LANES), 0) - lax.broadcasted_iota(jnp.int32, (LANES, LANES), 1)
+    ).astype(F32)
+    col_gap = col_gap * col_gap
+    grid[...] = jnp.zeros_like(grid)
+
+    @pl.loop(0, grid_rows)
+    def _(gap):
+        row_gap = gap.astype(F32)
+        distance = jnp.sqrt(row_gap * row_gap + col_gap)
+        block = (jnp.exp(-distance / LSCALE) / (8.0 * LSCALE)).astype(BF16)
+        toeplitz[grid_rows - 1 - gap] = block
+        toeplitz[grid_rows - 1 + gap] = block
+
     pl.semaphore_wait(barrier, len(peers))
 
     sent = []
@@ -433,9 +447,9 @@
 
     az_copies, ap_copies, ac_copies, cz_copies, cy_copies = {}, {}, {}, {}, {}
 
-    def forward_plane(src, k):
-        for j, shift in enumerate(plane):
-            if j:
+    def forward_plane(src, k, ways):
+        for j, shift in reversed(list(enumerate(plane))):
+            if j in ways:
                 ap_copies[j, k] = go(remote(src, block_of((0, 0), k), ap, j * n_z + k, plane_peer(shift)))
 
     def forward_core(src, j, k):
@@ -443,7 +457,7 @@
 
     for k in range(1, n_z):
         az_copies[k] = go(remote(duals_ref, block_of((0, 0), 0), az, k, z_peer(k)))
-    forward_plane(duals_ref, 0)
+    forward_plane(duals_ref, 0, (1, 2))
     forward_core(duals_ref, 0, 0)
     for k in range(1, n_z):
         cz_copies[k] = go(remote(coords_ref, coords_all.at[cell], cz, k, z_peer(k)))
@@ -484,10 +498,13 @@
                 fillers.pop(0)()
 
     fill(PLAN[0])
+    ap_copies[1, 0].wait_recv()
+    forward_plane(duals_ref, 0, (3,))
+    forward_core(block_of(plane[1], 0), 1, 0)
     for k in range(1, n_z):
         az_copies[k].wait_recv()
         src = block_of((0, 0), k)
-        forward_plane(src, k)
+        forward_plane(src, k, (1, 2, 3))
         forward_core(src, 0, k)
     for k in range(1, n_z):
         cz_copies[k].wait_recv()
@@ -497,8 +514,9 @@
     fill(PLAN[1])
     for k in range(n_z):
         for j in range(1, len(plane)):
-            ap_copies[j, k].wait_recv()
-            forward_core(block_of(plane[j], k), j, k)
+            if (j, k) != (1, 0):
+                ap_copies[j, k].wait_recv()
+                forward_core(block_of(plane[j], k), j, k)
     fill(PLAN[2])
     for k in range(n_z):
         for j in range(len(plane)):
@@ -529,20 +547,6 @@
         halves[k] = coords_all[k, 0:1, :] >> 1
         duo = lax.broadcasted_iota(jnp.int32, (duos * TILE, cells), 0) // TILE
         row_hot[k] = jnp.where(duo == halves[k], 1.0, 0.0).astype(BF16)
-    col_gap = (
-        lax.broadcasted_iota(jnp.int32, (LANES, LANES), 0) - lax.broadcasted_iota(jnp.int32, (LANES, LANES), 1)
-    ).astype(F32)
-    col_gap = col_gap * col_gap
-    grid[...] = jnp.zeros_like(grid)
-
-    @pl.loop(0, grid_rows)
-    def _(gap):
-        row_gap = gap.astype(F32)
-        distance = jnp.sqrt(row_gap * row_gap + col_gap)
-        block = (jnp.exp(-distance / LSCALE) / (8.0 * LSCALE)).astype(BF16)
-        toeplitz[grid_rows - 1 - gap] = block
-        toeplitz[grid_rows - 1 + gap] = block
-
     fill(PLAN[3])
 
     for i, c in reversed(list(enumerate(far_cells))):
@@ -626,13 +630,17 @@
         at = pl.ds(pl.multiple_of((t * n_cell + 2 * d) * rows, deep), deep)
         return jnp.dot(picked[at, :], weighted[...], preferred_element_type=F32).reshape(2, rows, reals)
 
+    def chunk_z(i):
+        between = 0 if i == 0 else jnp.where(i < z, i, i + 1)
+        return jnp.where(z == 0, n_z - 1 - i, z if i == n_z - 1 else between)
+
     dp_copies, dx_copies = {}, {}
     for d in range(n_z):
         for h in range(n_hi):
-            core_out[d, h] = product(h * 2 + (1 - core), d).astype(BF16)
+            core_out[d, h] = product(h * 2 + (1 - core), chunk_z(d)).astype(BF16)
         dp_copies[d] = go(remote(core_out.at[d], core_in.at[d], dp, d, partner))
     for d in range(n_z):
-        terms = [product(h * 2 + core, d) for h in range(n_hi)]
+        terms = [product(h * 2 + core, chunk_z(d)) for h in range(n_hi)]
         dp_copies[d].wait_recv()
         for h in range(n_hi):
             total = terms[h] + core_in[d, h].astype(F32)
@@ -644,15 +652,12 @@
                 for j in (1,):
                     dx_copies[j, 0].wait_recv()
 
-        for j, shift in enumerate(plane):
+        for j, shift in reversed(list(enumerate(plane))):
             if j:
                 src = plane_out.at[d, lax.rem(hi + shift[0], n_hi), y_in(shift)]
                 dx_copies[j, d] = go(
                     remote(src, plane_in.at[d, j], dx, j * n_z + d, plane_peer(shift))
                 )
-
-    def z_copy(d, at):
-        return remote(z_out.at[d], z_in.at[at], dz, at, (tm, d * 2 + y))
 
     for d in range(n_z):
         part = sums[d, hi, y]
@@ -666,28 +671,22 @@
             if d != 0 or j not in (1,):
                 dx_copies[j, d].wait_recv()
             part += plane_in[d, j].astype(F32)
-        sums[d, 0, 0] = part
-        z_out[d] = part.astype(BF16)
-
-        @pl.when(z != d)
-        def _():
-            z_copy(d, z).start()
-
-    result = sums[z, 0, 0]
-    for k in range(1, n_z):
-        z_copy(z_at(k), z_at(k)).wait_recv()
-        result += z_in[z_at(k)].astype(F32)
+        if d < n_z - 1:
+            z_out[d] = part.astype(BF16)
+            go(swap(z_out.at[d], z_in.at[z], dz, d, z, (tm, chunk_z(d) * 2 + y)))
+
+    result = part
+    for i in range(1, n_z):
+        there = z_at(i)
+        swap(z_out.at[0], z_in.at[there], dz, 0, there, (tm, there * 2 + y)).wait_recv()
+        result += z_in[there].astype(F32)
     out_ref[...] = result
 
     for copy in sent:
         copy.wait_send()
-    for d in range(n_z):
-        @pl.when(z != d)
-        def _():
-            z_copy(d, z).wait_send()
-
-
-PLAN = (0, 1, 0, 1)
+
+
+PLAN = (0, 1, 0, 2)
 
 
 def field_program(n_tm, n_cell, sensitivity, duals, time_cov, cell_coords, obs_time, obs_owner):

time: 39.7 us -> 39.3 us (0.990)
  Pallas kernels: 38.9 us -> 38.5 us
    pallas_call x1, Pallas kernels: 38.9 us -> 38.5 us  [field_program(): pl.pallas_call(functools.partial(field_kernel, (n_hi, n_cell)), out_shape...]
where the time goes in v5:
time: 39.3 us; the launch traced here: 39.1 us
  Pallas kernels  38.5 us (98%)
  local copies, waits for them, and re-layouts  0.62 us (2%)
    pallas_call x1, Pallas kernels, field_program(): pl.pallas_call(functools.partial(field_kernel, (n_hi, n_cell)), out_shape...  38.5 us

profile of v5, /device:TPU:0, one launch (start us, length us, event | category | flops | bytes accessed | tf_op | source)
XLA Modules:
  0.0 39.1 jit_solution(11758279524584362680)
XLA Ops:
  0.0 38.5 %shard_map.64 = f32[64,128]{1,0:T(8,128)S(1)} custom-call(bf16[2048,512]{1,0:T(8,128)(2,1)} %bitcast.3, bf16[64,128]{1,0:T(8,128)(2,1)} %duals_hbm.1, f32[4,4]{1,0:T(4,128)} %cov_hbm.1, s32[2,512]{1,0:T(2,128)} %coords_hbm.1, s32[1,2048]{1,0:T(1,128)} %bitcast.4, s32[1,2048]{1,0:T(1,128)} %bitcast.5), custom_call_target="tpu_custom_call" | custom-call | tf_op jit(solution)/shard_map/pallas_call | solution.py:705
  38.5 0.6 %copy.8 = f32[64,128]{1,0:T(8,128)} copy(f32[64,128]{1,0:T(8,128)S(1)} %shard_map.64) | data formatting | bytes 65536

commit v6 on v5

--- a/solution.py
+++ b/solution.py
@@ -522,9 +522,11 @@
         for j in range(len(plane)):
             ac_copies[j, k].wait_recv()
 
-    adjoint = jnp.dot(mask_t[...], full[...].reshape(obs, reals), preferred_element_type=F32)
-    for b in range(blocks):
-        stage[pl.ds(b, reals, stride=blocks), :] = adjoint[b * LANES:(b + 1) * LANES, :].T
+    everything = full[...].reshape(obs, reals)
+    for b in range(0, blocks, 2):
+        adjoint = jnp.dot(mask_t[b * LANES:(b + 2) * LANES, :], everything, preferred_element_type=F32)
+        for i in range(2):
+            stage[pl.ds(b + i, reals, stride=blocks), :] = adjoint[i * LANES:(i + 1) * LANES, :].T
     tiles[...] = stage[...].astype(BF16).reshape(tiles.shape)
 
     last = len(far_cells) - 1

time: 39.3 us -> 38.6 us (0.982)
  Pallas kernels: 38.5 us -> 37.8 us
    pallas_call x1, Pallas kernels: 38.5 us -> 37.8 us  [field_program(): pl.pallas_call(functools.partial(field_kernel, (n_hi, n_cell)), out_shape...]
where the time goes in v6:
time: 38.6 us; the launch traced here: 38.4 us
  Pallas kernels  37.8 us (98%)
  local copies, waits for them, and re-layouts  0.62 us (2%)
    pallas_call x1, Pallas kernels, field_program(): pl.pallas_call(functools.partial(field_kernel, (n_hi, n_cell)), out_shape...  37.8 us

profile of v6, /device:TPU:0, one launch (start us, length us, event | category | flops | bytes accessed | tf_op | source)
XLA Modules:
  0.0 38.4 jit_solution(15196462379653335618)
XLA Ops:
  0.0 37.8 %shard_map.64 = f32[64,128]{1,0:T(8,128)S(1)} custom-call(bf16[2048,512]{1,0:T(8,128)(2,1)} %bitcast.3, bf16[64,128]{1,0:T(8,128)(2,1)} %duals_hbm.1, f32[4,4]{1,0:T(4,128)} %cov_hbm.1, s32[2,512]{1,0:T(2,128)} %coords_hbm.1, s32[1,2048]{1,0:T(1,128)} %bitcast.4, s32[1,2048]{1,0:T(1,128)} %bitcast.5), custom_call_target="tpu_custom_call" | custom-call | tf_op jit(solution)/shard_map/pallas_call | solution.py:707
  37.8 0.6 %copy.8 = f32[64,128]{1,0:T(8,128)} copy(f32[64,128]{1,0:T(8,128)S(1)} %shard_map.64) | data formatting | bytes 65536

commit v7 on v6

--- a/solution.py
+++ b/solution.py
@@ -628,9 +628,13 @@
 
     deep = 2 * rows
 
-    def product(t, d):
-        at = pl.ds(pl.multiple_of((t * n_cell + 2 * d) * rows, deep), deep)
-        return jnp.dot(picked[at, :], weighted[...], preferred_element_type=F32).reshape(2, rows, reals)
+    def product(c, d):
+        picks = []
+        for h in range(n_hi):
+            at = pl.ds(pl.multiple_of(((h * 2 + c) * n_cell + 2 * d) * rows, deep), deep)
+            picks.append(picked[at, :])
+        out = jnp.dot(jnp.concatenate(picks, axis=0), weighted[...], preferred_element_type=F32)
+        return out.reshape(n_hi, 2, rows, reals)
 
     def chunk_z(i):
         between = 0 if i == 0 else jnp.where(i < z, i, i + 1)
@@ -638,11 +642,10 @@
 
     dp_copies, dx_copies = {}, {}
     for d in range(n_z):
-        for h in range(n_hi):
-            core_out[d, h] = product(h * 2 + (1 - core), chunk_z(d)).astype(BF16)
+        core_out[d] = product(1 - core, chunk_z(d)).astype(BF16)
         dp_copies[d] = go(remote(core_out.at[d], core_in.at[d], dp, d, partner))
     for d in range(n_z):
-        terms = [product(h * 2 + core, chunk_z(d)) for h in range(n_hi)]
+        terms = product(core, chunk_z(d))
         dp_copies[d].wait_recv()
         for h in range(n_hi):
             total = terms[h] + core_in[d, h].astype(F32)

time: 38.6 us -> 38.6 us (level)
  no operation moved by 1% of the time
where the time goes in v7:
time: 38.6 us; the launch traced here: 38.4 us
  Pallas kernels  37.8 us (98%)
  local copies, waits for them, and re-layouts  0.62 us (2%)
    pallas_call x1, Pallas kernels, field_program(): pl.pallas_call(functools.partial(field_kernel, (n_hi, n_cell)), out_shape...  37.8 us

profile of v7, /device:TPU:0, one launch (start us, length us, event | category | flops | bytes accessed | tf_op | source)
XLA Modules:
  0.0 38.4 jit_solution(6545782134780850573)
XLA Ops:
  0.0 37.8 %shard_map.64 = f32[64,128]{1,0:T(8,128)S(1)} custom-call(bf16[2048,512]{1,0:T(8,128)(2,1)} %bitcast.3, bf16[64,128]{1,0:T(8,128)(2,1)} %duals_hbm.1, f32[4,4]{1,0:T(4,128)} %cov_hbm.1, s32[2,512]{1,0:T(2,128)} %coords_hbm.1, s32[1,2048]{1,0:T(1,128)} %bitcast.4, s32[1,2048]{1,0:T(1,128)} %bitcast.5), custom_call_target="tpu_custom_call" | custom-call | tf_op jit(solution)/shard_map/pallas_call | solution.py:710
  37.8 0.6 %copy.8 = f32[64,128]{1,0:T(8,128)} copy(f32[64,128]{1,0:T(8,128)S(1)} %shard_map.64) | data formatting | bytes 65536
